TPU v7x, 32 devices: a whole 2x2x4 slice. The times are simulated.
32 devices in a mesh: outer: 8 (over z, x), inner: 4 (over y, core).
Axes of the slice: x: 2, y: 2, z: 4, core: 2. Of those that a mesh axis runs over, the one named last changes fastest.
Arguments:
- fine_input: bfloat16 [6144, 2048], P(('outer', 'inner')), may hold values from -12 to 12
- fine_query: bfloat16 [6144, 1024], P(('outer', 'inner')), may hold values from -4.5 to 4.5
- fine_key: bfloat16 [6144, 1024], P(('outer', 'inner')), may hold values from -4.5 to 4.5
- fine_value: bfloat16 [6144, 1024], P(('outer', 'inner')), may hold values from -6 to 6
- w_fine_out: bfloat16 [1024, 2048], P(None, 'inner'), may hold values from -0.1875 to 0.1875
- norm_gain: float32 [2048], replicated, may hold values from 0.25 to 1.75
- w_query: bfloat16 [2048, 512], P(None, 'inner'), may hold values from -1 to 1
- w_key: bfloat16 [2048, 512], P(None, 'inner'), may hold values from -1 to 1
- w_value: bfloat16 [2048, 512], P(None, 'inner'), may hold values from -0.125 to 0.125
- w_coarse_out: bfloat16 [512, 2048], P('inner'), may hold values from -0.25 to 0.25
Outputs:
- mixed_stream: bfloat16 [6144, 2048], P(('outer', 'inner'))
All inputs are finite; a program needn't handle non-finite values.
Results may differ from a plain program's by a relative error of at most 0.008.
Values may be sent and summed in bfloat16 or wider, within the bound.
No kernel may reach another device: no remote copies, remote signals or barrier semaphores. Data moves between devices by JAX's collectives and lax.ppermute only.
A program may use at most 128 MiB of HBM per device.

v0:
```python
import math
import jax
import jax.numpy as jnp
from jax import lax
from jax.sharding import PartitionSpec as P

HE = 128
WIN = 512
POOL = 8
very_negative = -1e30


def passed_along(block, axis, distance):
    devices = range(lax.axis_size(axis))
    route = [(i - distance, i) for i in devices if i - distance in devices]
    return lax.ppermute(block, axis, route)


def on_device(
    fine_input,
    fine_query,
    fine_key,
    fine_value,
    w_fine_out,
    norm_gain,
    w_query,
    w_key,
    w_value,
    w_coarse_out,
):
    tok_rows, model_width = fine_input.shape
    fine_heads = fine_query.shape[1] // HE
    score_scale = 1.0 / math.sqrt(HE)
    reach_count = (WIN + tok_rows - 1) // tok_rows
    position = lax.axis_index(("outer", "inner"))
    key_list = []
    value_list = []
    for distance in range(reach_count, 0, -1):
        shifted = passed_along((fine_key, fine_value), ("outer", "inner"), distance)
        key_list.append(shifted[0])
        value_list.append(shifted[1])
    key_list.append(fine_key)
    value_list.append(fine_value)
    span = (reach_count + 1) * tok_rows
    key_heads = jnp.concatenate(key_list, axis=0).reshape(span, fine_heads, HE)
    value_heads = jnp.concatenate(value_list, axis=0).reshape(span, fine_heads, HE)
    query_heads = fine_query.reshape(tok_rows, fine_heads, HE)
    scores = (
        jnp.einsum("qhe,khe->hqk", query_heads, key_heads, preferred_element_type=jnp.float32)
        * score_scale
    )
    row_ids = jnp.arange(tok_rows, dtype=jnp.int32)[:, None] + reach_count * tok_rows
    col_ids = jnp.arange(span, dtype=jnp.int32)[None, :]
    gap_rows = row_ids - col_ids
    allowed = (
        (gap_rows >= 0) & (gap_rows < WIN) & ((position - reach_count) * tok_rows + col_ids >= 0)
    )
    masked = jnp.where(allowed[None], scores, very_negative)
    row_max = jnp.max(masked, axis=-1, keepdims=True)
    exp_weights = jnp.where(allowed[None], jnp.exp(scores - row_max), 0.0)
    row_sum = jnp.sum(exp_weights, axis=-1)
    summed = jnp.einsum(
        "hqk,khe->qhe",
        exp_weights.astype(jnp.bfloat16),
        value_heads,
        preferred_element_type=jnp.float32,
    )
    fine_mix = (
        (summed / jnp.transpose(row_sum)[:, :, None])
        .astype(jnp.bfloat16)
        .reshape(tok_rows, fine_heads * HE)
    )
    projected = jnp.dot(
        fine_mix,
        lax.all_gather(w_fine_out, "inner", axis=1, tiled=True),
        preferred_element_type=jnp.float32,
    )
    fine_state = (fine_input.astype(jnp.float32) + projected).astype(jnp.bfloat16)
    edge_rows = passed_along(fine_state[tok_rows - POOL + 1 :], ("outer", "inner"), 1)
    first_pool = (
        jnp.sum(edge_rows, axis=0, dtype=jnp.float32) + fine_state[0].astype(jnp.float32)
    ) / POOL
    later_pools = (
        jnp.sum(
            fine_state[1 : tok_rows - POOL + 1].reshape(tok_rows // POOL - 1, POOL, model_width),
            axis=1,
            dtype=jnp.float32,
        )
        / POOL
    )
    pooled = jnp.concatenate([first_pool[None], later_pools], axis=0).astype(jnp.bfloat16)
    pooled_wide = pooled.astype(jnp.float32)
    moment = jnp.mean(pooled_wide * pooled_wide, axis=-1, keepdims=True)
    normed = (pooled_wide * lax.rsqrt(moment + 1e-06) * norm_gain).astype(jnp.bfloat16)
    local_heads = w_query.shape[1] // HE
    head_width = local_heads * HE
    joined_weights = jnp.concatenate([w_query, w_key, w_value], axis=1)
    projections = jnp.dot(
        lax.all_gather(normed, "inner", axis=0, tiled=True),
        joined_weights,
        preferred_element_type=jnp.float32,
    ).astype(jnp.bfloat16)
    group_len = projections.shape[0]
    coarse_query = projections[:, :head_width].reshape(group_len, local_heads, HE)
    coarse_key = projections[:, head_width : 2 * head_width]
    coarse_value = projections[:, 2 * head_width :]
    outer_index = lax.axis_index("outer")
    query_pos = outer_index * group_len + jnp.arange(group_len, dtype=jnp.int32)
    pieces = (
        lax.all_gather(coarse_key, "outer", axis=0, tiled=True),
        lax.all_gather(coarse_value, "outer", axis=0, tiled=True),
    )
    prior_max = jnp.full((local_heads, group_len), very_negative, jnp.float32)
    count = pieces[0].shape[0]
    block_keys = pieces[0].reshape(count, local_heads, HE)
    block_values = pieces[1].reshape(count, local_heads, HE)
    block_scores = (
        jnp.einsum("qhe,khe->hqk", coarse_query, block_keys, preferred_element_type=jnp.float32)
        * score_scale
    )
    key_pos = jnp.arange(count, dtype=jnp.int32)
    visible = (key_pos[None, :] <= query_pos[:, None])[None]
    block_masked = jnp.where(visible, block_scores, very_negative)
    new_max = jnp.maximum(prior_max, jnp.max(block_masked, axis=-1))
    block_exp = jnp.where(visible, jnp.exp(block_scores - new_max[:, :, None]), 0.0)
    new_sum = jnp.sum(block_exp, axis=-1)
    contrib = jnp.einsum(
        "hqk,khe->hqe",
        block_exp.astype(jnp.bfloat16),
        block_values,
        preferred_element_type=jnp.float32,
    )
    coarse_mix = (
        jnp.transpose(contrib / new_sum[:, :, None], (1, 0, 2))
        .reshape(group_len, head_width)
        .astype(jnp.bfloat16)
    )
    head_total = lax.psum_scatter(
        jnp.dot(coarse_mix, w_coarse_out, preferred_element_type=jnp.float32).astype(jnp.bfloat16),
        "inner",
        scatter_dimension=0,
        tiled=True,
    ).astype(jnp.float32)
    coarse_out = (pooled_wide + head_total).astype(jnp.bfloat16)
    fine_groups = fine_state.reshape(tok_rows // POOL, POOL, model_width).astype(jnp.float32)
    lifted = fine_groups + coarse_out.astype(jnp.float32)[:, None, :]
    return lifted.reshape(tok_rows, model_width).astype(jnp.bfloat16)


def solution(mesh):
    placed = (
        P(("outer", "inner"), None),
        P(("outer", "inner"), None),
        P(("outer", "inner"), None),
        P(("outer", "inner"), None),
        P(None, "inner"),
        P(),
        P(None, "inner"),
        P(None, "inner"),
        P(None, "inner"),
        P("inner", None),
    )
    return jax.shard_map(
        on_device,
        mesh=mesh,
        in_specs=placed,
        out_specs=P(("outer", "inner"), None),
        check_vma=False,
    )
```

profile of v0, /device:TPU:0, one launch (start us, length us, event | category | flops | bytes accessed | tf_op | source)
XLA Modules:
  0.0 202.3 jit_solution(12393071811701069702)
XLA Ops:
  6.5 0.0 copy-start
  6.5 0.0 all-gather.2.cloned.1.call-start
  6.5 0.7 all-gather.2.cloned.1.call-update
  7.3 0.0 reduce-scatter.2.cloned.1.call-start
  7.3 1.2 copy.16
  8.5 4.4 %collective-permute-start.3 = (bf16[192,1024]{0,1:T(8,128)(2,1)S(1)}, bf16[192,1024]{0,1:T(8,128)(2,1)S(1)}, u32[]{:S(2)}, u32[]{:S(2)}) collective-permute-start(bf16[192,1024]{0,1:T(8,128)(2,1)S(1)} %copy.16), channel_id=1, source_target_pairs={{0,3},{1,4},{2,5},{3,6},{4,7},{5,8},{6,9},{7,10},{8,11},{9,12},{10... | collective-permute-start | bytes 1179656 | tf_op jit(solution)/shard_map/ppermute | solution.py:16
  12.9 3.4 %collective-permute-start.4 = (bf16[192,1024]{0,1:T(8,128)(2,1)S(1)}, bf16[192,1024]{0,1:T(8,128)(2,1)S(1)}, u32[]{:S(2)}, u32[]{:S(2)}) collective-permute-start(bf16[192,1024]{0,1:T(8,128)(2,1)S(1)} %copy.16), channel_id=1, source_target_pairs={{0,2},{1,3},{2,4},{3,5},{4,6},{5,7},{6,8},{7,9},{8,10},{9,11},{10,... | collective-permute-start | bytes 1179656 | tf_op jit(solution)/shard_map/ppermute | solution.py:16
  16.3 3.1 %collective-permute-start.5 = (bf16[192,1024]{0,1:T(8,128)(2,1)S(1)}, bf16[192,1024]{0,1:T(8,128)(2,1)}, u32[]{:S(2)}, u32[]{:S(2)}) collective-permute-start(bf16[192,1024]{0,1:T(8,128)(2,1)S(1)} %copy.16), channel_id=1, source_target_pairs={{0,1},{1,2},{2,3},{3,4},{4,5},{5,6},{6,7},{7,8},{8,9},{9,10},{10,1... | collective-permute-start | bytes 1179656 | tf_op jit(solution)/shard_map/ppermute | solution.py:16
  19.4 1.2 copy.12
  20.6 4.2 %collective-permute-start = (bf16[192,1024]{0,1:T(8,128)(2,1)S(1)}, bf16[192,1024]{0,1:T(8,128)(2,1)}, u32[]{:S(2)}, u32[]{:S(2)}) collective-permute-start(bf16[192,1024]{0,1:T(8,128)(2,1)S(1)} %copy.12), channel_id=1, source_target_pairs={{0,3},{1,4},{2,5},{3,6},{4,7},{5,8},{6,9},{7,10},{8,11},{9,12},{10... | collective-permute-start | bytes 1179656 | tf_op jit(solution)/shard_map/ppermute | solution.py:16
  24.8 4.2 %collective-permute-start.1 = (bf16[192,1024]{0,1:T(8,128)(2,1)S(1)}, bf16[192,1024]{0,1:T(8,128)(2,1)}, u32[]{:S(2)}, u32[]{:S(2)}) collective-permute-start(bf16[192,1024]{0,1:T(8,128)(2,1)S(1)} %copy.12), channel_id=1, source_target_pairs={{0,2},{1,3},{2,4},{3,5},{4,6},{5,7},{6,8},{7,9},{8,10},{9,11},{10,... | collective-permute-start | bytes 1179656 | tf_op jit(solution)/shard_map/ppermute | solution.py:16
  29.1 0.0 collective-permute-done.3
  29.1 0.0 copy-start.2
  29.1 1.3 collective-permute-start.2
  30.4 0.2 fusion.37
  30.6 16.0 %collective-permute-done.4 = bf16[192,1024]{0,1:T(8,128)(2,1)S(1)} collective-permute-done((bf16[192,1024]{0,1:T(8,128)(2,1)S(1)}, bf16[192,1024]{0,1:T(8,128)(2,1)S(1)}, u32[]{:S(2)}, u32[]{:S(2)}) %collective-permute-start.4) | collective-permute-done | bytes 393248 | tf_op jit(solution)/shard_map/ppermute | solution.py:16
  46.7 0.8 copy-done.3
  47.4 0.0 collective-permute-done.5
  47.5 2.1 %pad_maximum_fusion.1 = bf16[768,1024]{0,1:T(8,128)(2,1)S(1)} fusion(bf16[192,1024]{0,1:T(8,128)(2,1)S(1)} %copy.16, bf16[192,1024]{0,1:T(8,128)(2,1)} %collective-permute-done.5, bf16[192,1024]{0,1:T(8,128)(2,1)} %copy-done.3, bf16[192,1024]{0,1:T(8,128)(2,1)} %copy-done.2), kind=kLoop, calls=%fused_computation.16 | loop fusion | flops 6291456 | bytes 3145728 | tf_op jit(solution)/shard_map/concatenate | solution.py:45
  49.6 0.0 copy-start.8
  49.6 17.4 %collective-permute-done = bf16[192,1024]{0,1:T(8,128)(2,1)} collective-permute-done((bf16[192,1024]{0,1:T(8,128)(2,1)S(1)}, bf16[192,1024]{0,1:T(8,128)(2,1)}, u32[]{:S(2)}, u32[]{:S(2)}) %collective-permute-start) | collective-permute-done | bytes 393248 | tf_op jit(solution)/shard_map/ppermute | solution.py:16
  67.0 11.2 %collective-permute-done.1 = bf16[192,1024]{0,1:T(8,128)(2,1)} collective-permute-done((bf16[192,1024]{0,1:T(8,128)(2,1)S(1)}, bf16[192,1024]{0,1:T(8,128)(2,1)}, u32[]{:S(2)}, u32[]{:S(2)}) %collective-permute-start.1) | collective-permute-done | bytes 393248 | tf_op jit(solution)/shard_map/ppermute | solution.py:16
  78.2 0.0 collective-permute-done.2
  78.2 3.1 %pad_maximum_fusion = bf16[768,1024]{0,1:T(8,128)(2,1)} fusion(bf16[192,1024]{0,1:T(8,128)(2,1)S(1)} %copy.12, bf16[192,1024]{0,1:T(8,128)(2,1)S(1)} %collective-permute-done.2, bf16[192,1024]{0,1:T(8,128)(2,1)} %collective-permute-done.1, bf16[192,1024]{0,1:T(8,128)(2,1)} %collective-permute-done), kind=kLoop, calls=%fused_computation.15 | loop fusion | flops 6291456 | bytes 3145728 | tf_op jit(solution)/shard_map/concatenate | solution.py:46
  81.3 3.7 %fusion.79 = (f32[8,192]{1,0:T(8,128)S(1)}, bf16[8,192,768]{2,1,0:T(8,128)(2,1)}) fusion(pred[192,768]{1,0:T(8,128)(4,1)S(1)} %fusion.37, bf16[768,8,128]{0,2,1:T(8,128)(2,1)S(1)} %bitcast.70, bf16[192,1024]{1,0:T(8,128)(2,1)S(1)} %copy-done.8), kind=kOutput, calls=%fused_computation.83 | convolution fusion | flops 612238080 | bytes 4478976 | tf_op jit(solution)/shard_map/sub | solution.py:60
  85.0 3.0 %fusion.27 = bf16[8,24,8,128]{3,2,1,0:T(8,128)(2,1)S(1)} fusion(bf16[768,8,128]{0,2,1:T(8,128)(2,1)} %bitcast.71, bf16[8,192,768]{2,1,0:T(8,128)(2,1)} %get-tuple-element.8, f32[192,8]{0,1:T(8,128)S(1)} %bitcast.73), kind=kOutput, calls=%fused_computation.29 | convolution fusion | flops 302383104 | bytes 4331520 | tf_op jit(solution)/shard_map/hqk,khe->qhe/dot_general | solution.py:62
  88.0 0.0 copy-start.4
  88.0 0.0 copy-start.5
  88.0 0.0 all-gather.2.cloned.1.call-done
  88.1 0.0 copy-start.6
  88.1 0.0 copy-start.7
  88.1 3.3 %fusion.5 = bf16[192,2048]{1,0:T(8,128)(2,1)S(1)} fusion(bf16[1024,2048]{1,0:T(8,128)(2,1)} %all-gather.2.cloned.1.call-done, bf16[192,2048]{1,0:T(8,128)(2,1)S(1)} %copy-done.1, bf16[8,24,8,128]{3,2,1,0:T(8,128)(2,1)S(1)} %fusion.27), kind=kOutput, calls=%fused_computation.8 | convolution fusion | flops 806486016 | bytes 6160384 | tf_op jit(solution)/shard_map/dot_general | solution.py:73
  91.4 0.5 convert_reduce_fusion
  92.0 5.1 %collective-permute-start.6 = (bf16[7,2048]{1,0:T(8,128)(2,1)S(1)}, bf16[7,2048]{1,0:T(8,128)(2,1)S(1)}, u32[]{:S(2)}, u32[]{:S(2)}) collective-permute-start(bf16[7,2048]{1,0:T(8,128)(2,1)S(1)} %slice.24), channel_id=1, source_target_pairs={{0,1},{1,2},{2,3},{3,4},{4,5},{5,6},{6,7},{7,8},{8,9},{9,10},{10,1... | collective-permute-start | bytes 86024 | tf_op jit(solution)/shard_map/ppermute | solution.py:16
  97.1 0.8 collective-permute-done.6
  98.0 0.2 fusion.55
  98.2 0.1 fusion.57
  98.3 9.8 %all_gather.13 = bf16[96,2048]{1,0:T(8,128)(2,1)S(1)} all-gather(bf16[24,2048]{1,0:T(8,128)(2,1)S(1)} %fusion.57), channel_id=1, replica_groups=mesh['outer'=8,'inner'=4] {'inner'}, dimensions={0}, use_global_device_ids=true | all-gather | bytes 491520 | tf_op jit(solution)/shard_map/all_gather | solution.py:99
  108.1 0.4 fusion.30
  108.5 31.0 %all_gather.14 = bf16[768,128]{1,0:T(8,128)(2,1)S(1)} all-gather(bf16[96,128]{1,0:T(8,128)(2,1)S(1)} %get-tuple-element.5), channel_id=1, replica_groups=mesh['outer'=8,'inner'=4] {'outer'}, dimensions={0}, use_global_device_ids=true | all-gather | bytes 221184 | tf_op jit(solution)/shard_map/all_gather | solution.py:110
  139.5 0.3 select_reduce_fusion
  139.9 30.6 %all_gather.15 = bf16[768,128]{1,0:T(8,128)(2,1)S(1)} all-gather(bf16[96,128]{1,0:T(8,128)(2,1)S(1)} %get-tuple-element.6), channel_id=1, replica_groups=mesh['outer'=8,'inner'=4] {'outer'}, dimensions={0}, use_global_device_ids=true | all-gather | bytes 221184 | tf_op jit(solution)/shard_map/all_gather | solution.py:111
  170.5 0.2 fusion.53
  170.7 1.2 convolution_convert_fusion
  171.9 0.0 reduce-scatter.2.cloned.1.call-update
  172.0 21.5 %reduce-scatter.2.cloned.1.call-done = bf16[24,2048]{1,0:T(8,128)(2,1)} async-done(((bf16[96,2048]{1,0:T(8,128)(2,1)}), bf16[24,2048]{1,0:T(8,128)(2,1)}) %reduce-scatter.2.cloned.1.call-update) | async-done | bytes 98320 | tf_op jit(solution)/shard_map/reduce_scatter | solution.py:138
  193.4 0.9 fusion.67
  194.4 1.1 fusion.17
  (20 shorter events, 0.1 us)
Async XLA Ops:
  6.5 164.2 %copy-start = (bf16[128,2048]{1,0:T(8,128)(2,1)S(1)}, bf16[128,2048]{1,0:T(8,128)(2,1)}, u32[]{:S(2)}) copy-start(bf16[128,2048]{1,0:T(8,128)(2,1)} %param.19) | copy-start | bytes 1572868
  6.5 81.5 %all-gather.2.cloned.1.call-start = ((), (), s32[]{:S(2)}) async-start(), calls=%async_computation.1 | async-start | bytes 5242880 | tf_op jit(solution)/shard_map/all_gather | solution.py:75
  7.3 186.2 %reduce-scatter.2.cloned.1.call-start = ((), (), s32[]{:S(2)}) async-start(), calls=%async_computation.2 | async-start | bytes 491520 | tf_op jit(solution)/shard_map/reduce_scatter | solution.py:138
  8.5 20.6 %collective-permute-start.3 = (bf16[192,1024]{0,1:T(8,128)(2,1)S(1)}, bf16[192,1024]{0,1:T(8,128)(2,1)S(1)}, u32[]{:S(2)}, u32[]{:S(2)}) collective-permute-start(bf16[192,1024]{0,1:T(8,128)(2,1)S(1)} %copy.16), channel_id=1, source_target_pairs={{0,3},{1,4},{2,5},{3,6},{4,7},{5,8},{6,9},{7,10},{8,11},{9,12},{10... | collective-permute-start | bytes 1179656 | tf_op jit(solution)/shard_map/ppermute | solution.py:16
  12.9 33.8 %collective-permute-start.4 = (bf16[192,1024]{0,1:T(8,128)(2,1)S(1)}, bf16[192,1024]{0,1:T(8,128)(2,1)S(1)}, u32[]{:S(2)}, u32[]{:S(2)}) collective-permute-start(bf16[192,1024]{0,1:T(8,128)(2,1)S(1)} %copy.16), channel_id=1, source_target_pairs={{0,2},{1,3},{2,4},{3,5},{4,6},{5,7},{6,8},{7,9},{8,10},{9,11},{10,... | collective-permute-start | bytes 1179656 | tf_op jit(solution)/shard_map/ppermute | solution.py:16
  16.3 31.2 %collective-permute-start.5 = (bf16[192,1024]{0,1:T(8,128)(2,1)S(1)}, bf16[192,1024]{0,1:T(8,128)(2,1)}, u32[]{:S(2)}, u32[]{:S(2)}) collective-permute-start(bf16[192,1024]{0,1:T(8,128)(2,1)S(1)} %copy.16), channel_id=1, source_target_pairs={{0,1},{1,2},{2,3},{3,4},{4,5},{5,6},{6,7},{7,8},{8,9},{9,10},{10,1... | collective-permute-start | bytes 1179656 | tf_op jit(solution)/shard_map/ppermute | solution.py:16
  20.6 46.3 %collective-permute-start = (bf16[192,1024]{0,1:T(8,128)(2,1)S(1)}, bf16[192,1024]{0,1:T(8,128)(2,1)}, u32[]{:S(2)}, u32[]{:S(2)}) collective-permute-start(bf16[192,1024]{0,1:T(8,128)(2,1)S(1)} %copy.12), channel_id=1, source_target_pairs={{0,3},{1,4},{2,5},{3,6},{4,7},{5,8},{6,9},{7,10},{8,11},{9,12},{10... | collective-permute-start | bytes 1179656 | tf_op jit(solution)/shard_map/ppermute | solution.py:16
  24.8 53.4 %collective-permute-start.1 = (bf16[192,1024]{0,1:T(8,128)(2,1)S(1)}, bf16[192,1024]{0,1:T(8,128)(2,1)}, u32[]{:S(2)}, u32[]{:S(2)}) collective-permute-start(bf16[192,1024]{0,1:T(8,128)(2,1)S(1)} %copy.12), channel_id=1, source_target_pairs={{0,2},{1,3},{2,4},{3,5},{4,6},{5,7},{6,8},{7,9},{8,10},{9,11},{10,... | collective-permute-start | bytes 1179656 | tf_op jit(solution)/shard_map/ppermute | solution.py:16
  29.1 17.6 %copy-start.2 = (bf16[192,1024]{0,1:T(8,128)(2,1)}, bf16[192,1024]{0,1:T(8,128)(2,1)S(1)}, u32[]{:S(2)}) copy-start(bf16[192,1024]{0,1:T(8,128)(2,1)S(1)} %collective-permute-done.3) | copy-start | bytes 1179652
  29.1 49.1 %collective-permute-start.2 = (bf16[192,1024]{0,1:T(8,128)(2,1)S(1)}, bf16[192,1024]{0,1:T(8,128)(2,1)S(1)}, u32[]{:S(2)}, u32[]{:S(2)}) collective-permute-start(bf16[192,1024]{0,1:T(8,128)(2,1)S(1)} %copy.12), channel_id=1, source_target_pairs={{0,1},{1,2},{2,3},{3,4},{4,5},{5,6},{6,7},{7,8},{8,9},{9,10},{10,1... | collective-permute-start | bytes 1179656 | tf_op jit(solution)/shard_map/ppermute | solution.py:16
  46.7 0.8 copy-start.3
  49.6 31.8 %copy-start.8 = (bf16[192,1024]{1,0:T(8,128)(2,1)S(1)}, bf16[192,1024]{1,0:T(8,128)(2,1)}, u32[]{:S(2)}) copy-start(bf16[192,1024]{1,0:T(8,128)(2,1)} %param.11) | copy-start | bytes 1179652
  85.0 3.0 %copy-start.1 = (bf16[192,2048]{1,0:T(8,128)(2,1)S(1)}, bf16[192,2048]{1,0:T(8,128)(2,1)}, u32[]{:S(2)}) copy-start(bf16[192,2048]{1,0:T(8,128)(2,1)} %param.10) | copy-start | bytes 2359300
  88.0 10.1 %copy-start.4 = (f32[2048]{0:T(1024)S(1)}, f32[2048]{0:T(1024)}, u32[]{:S(2)}) copy-start(f32[2048]{0:T(1024)} %param.15) | copy-start | bytes 24580
  88.0 20.0 %copy-start.5 = (bf16[2048,128]{1,0:T(8,128)(2,1)S(1)}, bf16[2048,128]{1,0:T(8,128)(2,1)}, u32[]{:S(2)}) copy-start(bf16[2048,128]{1,0:T(8,128)(2,1)} %param.18) | copy-start | bytes 1572868
  88.1 20.0 %copy-start.6 = (bf16[2048,128]{1,0:T(8,128)(2,1)S(1)}, bf16[2048,128]{1,0:T(8,128)(2,1)}, u32[]{:S(2)}) copy-start(bf16[2048,128]{1,0:T(8,128)(2,1)} %param.17) | copy-start | bytes 1572868
  88.1 20.0 %copy-start.7 = (bf16[2048,128]{1,0:T(8,128)(2,1)S(1)}, bf16[2048,128]{1,0:T(8,128)(2,1)}, u32[]{:S(2)}) copy-start(bf16[2048,128]{1,0:T(8,128)(2,1)} %param.16) | copy-start | bytes 1572868
  92.0 6.0 %collective-permute-start.6 = (bf16[7,2048]{1,0:T(8,128)(2,1)S(1)}, bf16[7,2048]{1,0:T(8,128)(2,1)S(1)}, u32[]{:S(2)}, u32[]{:S(2)}) collective-permute-start(bf16[7,2048]{1,0:T(8,128)(2,1)S(1)} %slice.24), channel_id=1, source_target_pairs={{0,1},{1,2},{2,3},{3,4},{4,5},{5,6},{6,7},{7,8},{8,9},{9,10},{10,1... | collective-permute-start | bytes 86024 | tf_op jit(solution)/shard_map/ppermute | solution.py:16
Sparse Core Ops, SparseCore 0:
  8.9 56.0 all-gather.1
  172.1 21.3 reduce-scatter.1
where the time goes:
time: 203 us; the launch traced here: 202 us
  blocking collectives  71.5 us (35%)
  waiting for transfers between devices  67.7 us (33%)
  starting transfers between devices  25.8 us (13%)
  between operations  13.6 us (7%)
  matrix products  11.9 us (6%)
  other arithmetic  8.52 us (4%)
  local copies, waits for them, and re-layouts  3.27 us (2%)
    ppermute x7, waiting for transfers between devices, passed_along(): return lax.ppermute(block, axis, route)  45.5 us
    all_gather x1, blocking collectives, on_device(): lax.all_gather(coarse_key, 'outer', axis=0, tiled=True)  31 us
    all_gather x1, blocking collectives, on_device(): lax.all_gather(coarse_value, 'outer', axis=0, tiled=True)  30.6 us
    ppermute x7, starting transfers between devices, passed_along(): return lax.ppermute(block, axis, route)  25.7 us
    reduce_scatter x1, waiting for transfers between devices, on_device(): lax.psum_scatter(jnp.dot(coarse_mix, w_coarse_out, preferred_element_type...  21.5 us
    all_gather x1, blocking collectives, on_device(): lax.all_gather(normed, 'inner', axis=0, tiled=True)  9.81 us
  transfers between devices with their start and end apart: 9, of which 5 were waited for; matrix products, arithmetic and copies ran while one was open for 7% of the time, Pallas kernels for 0%

commit v1 on v0

--- a/solution.py
+++ b/solution.py
@@ -8,6 +8,39 @@
 WIN = 512
 POOL = 8
 very_negative = -1e30
+
+
+def test_sums_all_here(tile_in, where_dim):
+    row_axis = "outer"
+    view_out = lax.axis_size(row_axis)
+    high = lax.axis_index(row_axis)
+    piece_out, z, passed = (view_out, high, tile_in.shape[where_dim])
+    far_arr = range(piece_out)
+    newest = map(lambda src_i: (src_i, (src_i + 1) % piece_out), far_arr)
+    kept_rows = list(newest)
+    b_now = range(piece_out)
+    frame_out = map(lambda src_i: (src_i, (src_i - 1) % piece_out), b_now)
+    rack = list(frame_out)
+    q_next = jnp.zeros(
+        (*tile_in.shape[:where_dim], piece_out * passed, *tile_in.shape[where_dim + 1 :]),
+        tile_in.dtype,
+    )
+    q_next = lax.dynamic_update_slice_in_dim(q_next, tile_in, z * passed, axis=where_dim)
+    t1 = fresh = tile_in
+    part_next = piece_out // 2
+    b = 1
+    while b < part_next + 1:
+        t1 = lax.ppermute(t1, row_axis, kept_rows)
+        q_next = lax.dynamic_update_slice_in_dim(
+            q_next, t1, (z - b) % piece_out * passed, axis=where_dim
+        )
+        if b < piece_out - part_next:
+            fresh = lax.ppermute(fresh, row_axis, rack)
+            q_next = lax.dynamic_update_slice_in_dim(
+                q_next, fresh, (z + b) % piece_out * passed, axis=where_dim
+            )
+        b = b + 1
+    return q_next
 
 
 def passed_along(block, axis, distance):
@@ -107,7 +140,7 @@
     outer_index = lax.axis_index("outer")
     query_pos = outer_index * group_len + jnp.arange(group_len, dtype=jnp.int32)
     pieces = (
-        lax.all_gather(coarse_key, "outer", axis=0, tiled=True),
+        test_sums_all_here(coarse_key, 0),
         lax.all_gather(coarse_value, "outer", axis=0, tiled=True),
     )
     prior_max = jnp.full((local_heads, group_len), very_negative, jnp.float32)

time: 203 us -> 193 us (0.951)
  blocking collectives: 71.5 us -> 40.6 us
  starting transfers between devices: 25.8 us -> 40.7 us
  waiting for transfers between devices: 67.7 us -> 74.2 us
    all_gather x1 -> x0, blocking collectives: 31 us -> none  [on_device(): lax.all_gather(coarse_key, 'outer', axis=0, tiled=True)]
    ppermute x0 -> x7, starting transfers between devices: none -> 14.2 us  [the longest x3 12.7 us: test_sums_all_here(): fresh = lax.ppermute(fresh, row_axis, rack)]
    ppermute x0 -> x7, waiting for transfers between devices: none -> 10.1 us  [the longest x4 10 us: test_sums_all_here(): t1 = lax.ppermute(t1, row_axis, kept_rows)]
    reduce_scatter x1, waiting for transfers between devices: 21.5 us -> 17.9 us  [on_device(): lax.psum_scatter(jnp.dot(coarse_mix, w_coarse_out, preferred_element_type...]
  transfers between devices with their start and end apart: 9 -> 16, of which waited for: 5 -> 8; matrix products, arithmetic and copies ran while one was open for 7% -> 8% of each run, Pallas kernels for 0% -> 0%
where the time goes in v1:
time: 193 us; the launch traced here: 192 us
  waiting for transfers between devices  74.2 us (38%)
  starting transfers between devices  40.7 us (21%)
  blocking collectives  40.6 us (21%)
  between operations  13.6 us (7%)
  matrix products  11.9 us (6%)
  other arithmetic  8.67 us (4%)
  local copies, waits for them, and re-layouts  2.66 us (1%)
    ppermute x7, waiting for transfers between devices, passed_along(): return lax.ppermute(block, axis, route)  45.5 us
    all_gather x1, blocking collectives, on_device(): lax.all_gather(coarse_value, 'outer', axis=0, tiled=True)  30.6 us
    ppermute x7, starting transfers between devices, passed_along(): return lax.ppermute(block, axis, route)  26.5 us
    reduce_scatter x1, waiting for transfers between devices, on_device(): lax.psum_scatter(jnp.dot(coarse_mix, w_coarse_out, preferred_element_type...  17.9 us
    ppermute x3, starting transfers between devices, test_sums_all_here(): fresh = lax.ppermute(fresh, row_axis, rack)  12.7 us
    ppermute x4, waiting for transfers between devices, test_sums_all_here(): t1 = lax.ppermute(t1, row_axis, kept_rows)  10 us
    all_gather x1, blocking collectives, on_device(): lax.all_gather(normed, 'inner', axis=0, tiled=True)  9.93 us
  transfers between devices with their start and end apart: 16, of which 8 were waited for; matrix products, arithmetic and copies ran while one was open for 8% of the time, Pallas kernels for 0%

profile of v1, /device:TPU:0, one launch (start us, length us, event | category | flops | bytes accessed | tf_op | source)
XLA Modules:
  0.0 192.4 jit_solution(14415354243574767826)
XLA Ops:
  6.5 0.7 all-gather.2.cloned.1.call-update
  7.3 0.0 reduce-scatter.2.cloned.1.call-start
  7.3 1.2 copy.16
  8.5 4.4 %collective-permute-start.3 = (bf16[192,1024]{0,1:T(8,128)(2,1)S(1)}, bf16[192,1024]{0,1:T(8,128)(2,1)S(1)}, u32[]{:S(2)}, u32[]{:S(2)}) collective-permute-start(bf16[192,1024]{0,1:T(8,128)(2,1)S(1)} %copy.16), channel_id=1, source_target_pairs={{0,3},{1,4},{2,5},{3,6},{4,7},{5,8},{6,9},{7,10},{8,11},{9,12},{10... | collective-permute-start | bytes 1179656 | tf_op jit(solution)/shard_map/ppermute | solution.py:49
  12.9 4.2 %collective-permute-start.4 = (bf16[192,1024]{0,1:T(8,128)(2,1)S(1)}, bf16[192,1024]{0,1:T(8,128)(2,1)}, u32[]{:S(2)}, u32[]{:S(2)}) collective-permute-start(bf16[192,1024]{0,1:T(8,128)(2,1)S(1)} %copy.16), channel_id=1, source_target_pairs={{0,2},{1,3},{2,4},{3,5},{4,6},{5,7},{6,8},{7,9},{8,10},{9,11},{10,... | collective-permute-start | bytes 1179656 | tf_op jit(solution)/shard_map/ppermute | solution.py:49
  17.0 3.1 %collective-permute-start.5 = (bf16[192,1024]{0,1:T(8,128)(2,1)S(1)}, bf16[192,1024]{0,1:T(8,128)(2,1)}, u32[]{:S(2)}, u32[]{:S(2)}) collective-permute-start(bf16[192,1024]{0,1:T(8,128)(2,1)S(1)} %copy.16), channel_id=1, source_target_pairs={{0,1},{1,2},{2,3},{3,4},{4,5},{5,6},{6,7},{7,8},{8,9},{9,10},{10,1... | collective-permute-start | bytes 1179656 | tf_op jit(solution)/shard_map/ppermute | solution.py:49
  20.2 1.3 copy.12
  21.5 3.4 %collective-permute-start = (bf16[192,1024]{0,1:T(8,128)(2,1)S(1)}, bf16[192,1024]{0,1:T(8,128)(2,1)}, u32[]{:S(2)}, u32[]{:S(2)}) collective-permute-start(bf16[192,1024]{0,1:T(8,128)(2,1)S(1)} %copy.12), channel_id=1, source_target_pairs={{0,3},{1,4},{2,5},{3,6},{4,7},{5,8},{6,9},{7,10},{8,11},{9,12},{10... | collective-permute-start | bytes 1179656 | tf_op jit(solution)/shard_map/ppermute | solution.py:49
  24.8 4.2 %collective-permute-start.1 = (bf16[192,1024]{0,1:T(8,128)(2,1)S(1)}, bf16[192,1024]{0,1:T(8,128)(2,1)}, u32[]{:S(2)}, u32[]{:S(2)}) collective-permute-start(bf16[192,1024]{0,1:T(8,128)(2,1)S(1)} %copy.12), channel_id=1, source_target_pairs={{0,2},{1,3},{2,4},{3,5},{4,6},{5,7},{6,8},{7,9},{8,10},{9,11},{10,... | collective-permute-start | bytes 1179656 | tf_op jit(solution)/shard_map/ppermute | solution.py:49
  29.1 0.0 copy-start.2
  29.1 2.1 %collective-permute-start.2 = (bf16[192,1024]{0,1:T(8,128)(2,1)S(1)}, bf16[192,1024]{0,1:T(8,128)(2,1)}, u32[]{:S(2)}, u32[]{:S(2)}) collective-permute-start(bf16[192,1024]{0,1:T(8,128)(2,1)S(1)} %copy.12), channel_id=1, source_target_pairs={{0,1},{1,2},{2,3},{3,4},{4,5},{5,6},{6,7},{7,8},{8,9},{9,10},{10,1... | collective-permute-start | bytes 1179656 | tf_op jit(solution)/shard_map/ppermute | solution.py:49
  31.2 0.2 fusion.37
  31.4 15.2 %collective-permute-done.4 = bf16[192,1024]{0,1:T(8,128)(2,1)} collective-permute-done((bf16[192,1024]{0,1:T(8,128)(2,1)S(1)}, bf16[192,1024]{0,1:T(8,128)(2,1)}, u32[]{:S(2)}, u32[]{:S(2)}) %collective-permute-start.4) | collective-permute-done | bytes 393248 | tf_op jit(solution)/shard_map/ppermute | solution.py:49
  46.7 2.1 %pad_maximum_fusion.1 = bf16[768,1024]{0,1:T(8,128)(2,1)S(1)} fusion(bf16[192,1024]{0,1:T(8,128)(2,1)S(1)} %copy.16, bf16[192,1024]{0,1:T(8,128)(2,1)} %collective-permute-done.5, bf16[192,1024]{0,1:T(8,128)(2,1)} %collective-permute-done.4, bf16[192,1024]{0,1:T(8,128)(2,1)} %copy-done.2), kind=kLoop, calls=%fused_computation.16 | loop fusion | flops 6291456 | bytes 3145728 | tf_op jit(solution)/shard_map/concatenate | solution.py:78
  48.8 0.0 copy-start.7
  48.8 18.2 %collective-permute-done = bf16[192,1024]{0,1:T(8,128)(2,1)} collective-permute-done((bf16[192,1024]{0,1:T(8,128)(2,1)S(1)}, bf16[192,1024]{0,1:T(8,128)(2,1)}, u32[]{:S(2)}, u32[]{:S(2)}) %collective-permute-start) | collective-permute-done | bytes 393248 | tf_op jit(solution)/shard_map/ppermute | solution.py:49
  67.0 11.2 %collective-permute-done.1 = bf16[192,1024]{0,1:T(8,128)(2,1)} collective-permute-done((bf16[192,1024]{0,1:T(8,128)(2,1)S(1)}, bf16[192,1024]{0,1:T(8,128)(2,1)}, u32[]{:S(2)}, u32[]{:S(2)}) %collective-permute-start.1) | collective-permute-done | bytes 393248 | tf_op jit(solution)/shard_map/ppermute | solution.py:49
  78.2 3.2 %pad_maximum_fusion = bf16[768,1024]{0,1:T(8,128)(2,1)} fusion(bf16[192,1024]{0,1:T(8,128)(2,1)S(1)} %copy.12, bf16[192,1024]{0,1:T(8,128)(2,1)} %collective-permute-done.2, bf16[192,1024]{0,1:T(8,128)(2,1)} %collective-permute-done.1, bf16[192,1024]{0,1:T(8,128)(2,1)} %collective-permute-done), kind=kLoop, calls=%fused_computation.15 | loop fusion | flops 6291456 | bytes 3145728 | tf_op jit(solution)/shard_map/concatenate | solution.py:79
  81.5 3.7 %fusion.79 = (f32[8,192]{1,0:T(8,128)S(1)}, bf16[8,192,768]{2,1,0:T(8,128)(2,1)}) fusion(pred[192,768]{1,0:T(8,128)(4,1)S(1)} %fusion.37, bf16[768,8,128]{0,2,1:T(8,128)(2,1)S(1)} %bitcast.70, bf16[192,1024]{1,0:T(8,128)(2,1)S(1)} %copy-done.7), kind=kOutput, calls=%fused_computation.91 | convolution fusion | flops 612238080 | bytes 4478976 | tf_op jit(solution)/shard_map/sub | solution.py:93
  85.2 3.0 %fusion.27 = bf16[8,24,8,128]{3,2,1,0:T(8,128)(2,1)S(1)} fusion(bf16[768,8,128]{0,2,1:T(8,128)(2,1)} %bitcast.71, bf16[8,192,768]{2,1,0:T(8,128)(2,1)} %get-tuple-element.9, f32[192,8]{0,1:T(8,128)S(1)} %bitcast.73), kind=kOutput, calls=%fused_computation.29 | convolution fusion | flops 302383104 | bytes 4331520 | tf_op jit(solution)/shard_map/hqk,khe->qhe/dot_general | solution.py:95
  88.2 0.0 copy-start.3
  88.2 0.0 all-gather.2.cloned.1.call-done
  88.2 0.0 copy-start.5
  88.2 0.0 copy-start.6
  88.2 3.3 %fusion.5 = bf16[192,2048]{1,0:T(8,128)(2,1)S(1)} fusion(bf16[1024,2048]{1,0:T(8,128)(2,1)} %all-gather.2.cloned.1.call-done, bf16[192,2048]{1,0:T(8,128)(2,1)S(1)} %copy-done.1, bf16[8,24,8,128]{3,2,1,0:T(8,128)(2,1)S(1)} %fusion.27), kind=kOutput, calls=%fused_computation.8 | convolution fusion | flops 806486016 | bytes 6160384 | tf_op jit(solution)/shard_map/dot_general | solution.py:106
  91.5 0.5 convert_reduce_fusion
  92.1 5.1 %collective-permute-start.6 = (bf16[7,2048]{1,0:T(8,128)(2,1)S(1)}, bf16[7,2048]{1,0:T(8,128)(2,1)S(1)}, u32[]{:S(2)}, u32[]{:S(2)}) collective-permute-start(bf16[7,2048]{1,0:T(8,128)(2,1)S(1)} %slice.24), channel_id=1, source_target_pairs={{0,1},{1,2},{2,3},{3,4},{4,5},{5,6},{6,7},{7,8},{8,9},{9,10},{10,1... | collective-permute-start | bytes 86024 | tf_op jit(solution)/shard_map/ppermute | solution.py:49
  97.3 0.8 collective-permute-done.6
  98.1 0.2 fusion.55
  98.3 0.1 fusion.57
  98.4 9.9 %all_gather.10 = bf16[96,2048]{1,0:T(8,128)(2,1)S(1)} all-gather(bf16[24,2048]{1,0:T(8,128)(2,1)S(1)} %fusion.57), channel_id=1, replica_groups=mesh['outer'=8,'inner'=4] {'inner'}, dimensions={0}, use_global_device_ids=true | all-gather | bytes 491520 | tf_op jit(solution)/shard_map/all_gather | solution.py:132
  108.3 0.4 fusion.30
  108.8 1.5 collective-permute-start.7
  110.4 3.2 %collective-permute-start.8 = (bf16[96,128]{1,0:T(8,128)(2,1)S(1)}, bf16[96,128]{1,0:T(8,128)(2,1)S(1)}, u32[]{:S(2)}, u32[]{:S(2)}) collective-permute-start(bf16[96,128]{1,0:T(8,128)(2,1)S(1)} %get-tuple-element.5), channel_id=1, source_target_pairs={{0,28},{4,0},{8,4},{12,8},{16,12},{20,16},{24,20},{28,24},{1,29},{... | collective-permute-start | bytes 73736 | tf_op jit(solution)/shard_map/ppermute | solution.py:38
  113.6 30.6 %all_gather.11 = bf16[768,128]{1,0:T(8,128)(2,1)S(1)} all-gather(bf16[96,128]{1,0:T(8,128)(2,1)S(1)} %get-tuple-element.7), channel_id=1, replica_groups=mesh['outer'=8,'inner'=4] {'outer'}, dimensions={0}, use_global_device_ids=true | all-gather | bytes 221184 | tf_op jit(solution)/shard_map/all_gather | solution.py:144
  144.2 0.0 collective-permute-start.9
  144.2 4.7 %collective-permute-start.10 = (bf16[96,128]{1,0:T(8,128)(2,1)S(1)}, bf16[96,128]{1,0:T(8,128)(2,1)S(1)}, u32[]{:S(2)}, u32[]{:S(2)}) collective-permute-start(bf16[96,128]{1,0:T(8,128)(2,1)S(1)} %collective-permute-done.8), channel_id=1, source_target_pairs={{0,28},{4,0},{8,4},{12,8},{16,12},{20,16},{24,20},{28,24},{1,29},{... | collective-permute-start | bytes 73736 | tf_op jit(solution)/shard_map/ppermute | solution.py:38
  149.0 1.8 collective-permute-done.9
  150.8 4.7 %collective-permute-start.12 = (bf16[96,128]{1,0:T(8,128)(2,1)S(1)}, bf16[96,128]{1,0:T(8,128)(2,1)S(1)}, u32[]{:S(2)}, u32[]{:S(2)}) collective-permute-start(bf16[96,128]{1,0:T(8,128)(2,1)S(1)} %collective-permute-done.10), channel_id=1, source_target_pairs={{0,28},{4,0},{8,4},{12,8},{16,12},{20,16},{24,20},{28,24},{1,29},{... | collective-permute-start | bytes 73736 | tf_op jit(solution)/shard_map/ppermute | solution.py:38
  155.5 1.8 collective-permute-done.11
  157.3 6.5 %collective-permute-done.13 = bf16[96,128]{1,0:T(8,128)(2,1)S(1)} collective-permute-done((bf16[96,128]{1,0:T(8,128)(2,1)S(1)}, bf16[96,128]{1,0:T(8,128)(2,1)S(1)}, u32[]{:S(2)}, u32[]{:S(2)}) %collective-permute-start.13) | collective-permute-done | bytes 24608 | tf_op jit(solution)/shard_map/ppermute | solution.py:33
  163.8 0.3 select_reduce_fusion
  164.1 0.2 fusion.53
  164.4 1.3 convolution_convert_fusion
  165.6 0.0 reduce-scatter.2.cloned.1.call-update
  165.6 17.9 %reduce-scatter.2.cloned.1.call-done = bf16[24,2048]{1,0:T(8,128)(2,1)} async-done(((bf16[96,2048]{1,0:T(8,128)(2,1)}), bf16[24,2048]{1,0:T(8,128)(2,1)}) %reduce-scatter.2.cloned.1.call-update) | async-done | bytes 98320 | tf_op jit(solution)/shard_map/reduce_scatter | solution.py:171
  183.6 0.9 fusion.67
  184.5 1.1 fusion.17
  (39 shorter events, 0.3 us)
Async XLA Ops:
  6.5 157.8 %copy-start = (bf16[128,2048]{1,0:T(8,128)(2,1)S(1)}, bf16[128,2048]{1,0:T(8,128)(2,1)}, u32[]{:S(2)}) copy-start(bf16[128,2048]{1,0:T(8,128)(2,1)} %param.19) | copy-start | bytes 1572868
  6.5 81.7 %all-gather.2.cloned.1.call-start = ((), (), s32[]{:S(2)}) async-start(), calls=%async_computation.1 | async-start | bytes 5242880 | tf_op jit(solution)/shard_map/all_gather | solution.py:108
  7.3 176.3 %reduce-scatter.2.cloned.1.call-start = ((), (), s32[]{:S(2)}) async-start(), calls=%async_computation.2 | async-start | bytes 491520 | tf_op jit(solution)/shard_map/reduce_scatter | solution.py:171
  8.5 20.6 %collective-permute-start.3 = (bf16[192,1024]{0,1:T(8,128)(2,1)S(1)}, bf16[192,1024]{0,1:T(8,128)(2,1)S(1)}, u32[]{:S(2)}, u32[]{:S(2)}) collective-permute-start(bf16[192,1024]{0,1:T(8,128)(2,1)S(1)} %copy.16), channel_id=1, source_target_pairs={{0,3},{1,4},{2,5},{3,6},{4,7},{5,8},{6,9},{7,10},{8,11},{9,12},{10... | collective-permute-start | bytes 1179656 | tf_op jit(solution)/shard_map/ppermute | solution.py:49
  12.9 33.8 %collective-permute-start.4 = (bf16[192,1024]{0,1:T(8,128)(2,1)S(1)}, bf16[192,1024]{0,1:T(8,128)(2,1)}, u32[]{:S(2)}, u32[]{:S(2)}) collective-permute-start(bf16[192,1024]{0,1:T(8,128)(2,1)S(1)} %copy.16), channel_id=1, source_target_pairs={{0,2},{1,3},{2,4},{3,5},{4,6},{5,7},{6,8},{7,9},{8,10},{9,11},{10,... | collective-permute-start | bytes 1179656 | tf_op jit(solution)/shard_map/ppermute | solution.py:49
  17.0 29.6 %collective-permute-start.5 = (bf16[192,1024]{0,1:T(8,128)(2,1)S(1)}, bf16[192,1024]{0,1:T(8,128)(2,1)}, u32[]{:S(2)}, u32[]{:S(2)}) collective-permute-start(bf16[192,1024]{0,1:T(8,128)(2,1)S(1)} %copy.16), channel_id=1, source_target_pairs={{0,1},{1,2},{2,3},{3,4},{4,5},{5,6},{6,7},{7,8},{8,9},{9,10},{10,1... | collective-permute-start | bytes 1179656 | tf_op jit(solution)/shard_map/ppermute | solution.py:49
  21.5 45.5 %collective-permute-start = (bf16[192,1024]{0,1:T(8,128)(2,1)S(1)}, bf16[192,1024]{0,1:T(8,128)(2,1)}, u32[]{:S(2)}, u32[]{:S(2)}) collective-permute-start(bf16[192,1024]{0,1:T(8,128)(2,1)S(1)} %copy.12), channel_id=1, source_target_pairs={{0,3},{1,4},{2,5},{3,6},{4,7},{5,8},{6,9},{7,10},{8,11},{9,12},{10... | collective-permute-start | bytes 1179656 | tf_op jit(solution)/shard_map/ppermute | solution.py:49
  24.8 53.4 %collective-permute-start.1 = (bf16[192,1024]{0,1:T(8,128)(2,1)S(1)}, bf16[192,1024]{0,1:T(8,128)(2,1)}, u32[]{:S(2)}, u32[]{:S(2)}) collective-permute-start(bf16[192,1024]{0,1:T(8,128)(2,1)S(1)} %copy.12), channel_id=1, source_target_pairs={{0,2},{1,3},{2,4},{3,5},{4,6},{5,7},{6,8},{7,9},{8,10},{9,11},{10,... | collective-permute-start | bytes 1179656 | tf_op jit(solution)/shard_map/ppermute | solution.py:49
  29.1 17.6 %copy-start.2 = (bf16[192,1024]{0,1:T(8,128)(2,1)}, bf16[192,1024]{0,1:T(8,128)(2,1)S(1)}, u32[]{:S(2)}) copy-start(bf16[192,1024]{0,1:T(8,128)(2,1)S(1)} %collective-permute-done.3) | copy-start | bytes 1179652
  29.1 49.1 %collective-permute-start.2 = (bf16[192,1024]{0,1:T(8,128)(2,1)S(1)}, bf16[192,1024]{0,1:T(8,128)(2,1)}, u32[]{:S(2)}, u32[]{:S(2)}) collective-permute-start(bf16[192,1024]{0,1:T(8,128)(2,1)S(1)} %copy.12), channel_id=1, source_target_pairs={{0,1},{1,2},{2,3},{3,4},{4,5},{5,6},{6,7},{7,8},{8,9},{9,10},{10,1... | collective-permute-start | bytes 1179656 | tf_op jit(solution)/shard_map/ppermute | solution.py:49
  48.8 32.7 %copy-start.7 = (bf16[192,1024]{1,0:T(8,128)(2,1)S(1)}, bf16[192,1024]{1,0:T(8,128)(2,1)}, u32[]{:S(2)}) copy-start(bf16[192,1024]{1,0:T(8,128)(2,1)} %param.11) | copy-start | bytes 1179652
  85.2 3.0 %copy-start.1 = (bf16[192,2048]{1,0:T(8,128)(2,1)S(1)}, bf16[192,2048]{1,0:T(8,128)(2,1)}, u32[]{:S(2)}) copy-start(bf16[192,2048]{1,0:T(8,128)(2,1)} %param.10) | copy-start | bytes 2359300
  88.2 10.1 %copy-start.3 = (f32[2048]{0:T(1024)S(1)}, f32[2048]{0:T(1024)}, u32[]{:S(2)}) copy-start(f32[2048]{0:T(1024)} %param.15) | copy-start | bytes 24580
  88.2 20.2 %copy-start.4 = (bf16[2048,128]{1,0:T(8,128)(2,1)S(1)}, bf16[2048,128]{1,0:T(8,128)(2,1)}, u32[]{:S(2)}) copy-start(bf16[2048,128]{1,0:T(8,128)(2,1)} %param.18) | copy-start | bytes 1572868
  88.2 20.1 %copy-start.5 = (bf16[2048,128]{1,0:T(8,128)(2,1)S(1)}, bf16[2048,128]{1,0:T(8,128)(2,1)}, u32[]{:S(2)}) copy-start(bf16[2048,128]{1,0:T(8,128)(2,1)} %param.17) | copy-start | bytes 1572868
  88.2 20.1 %copy-start.6 = (bf16[2048,128]{1,0:T(8,128)(2,1)S(1)}, bf16[2048,128]{1,0:T(8,128)(2,1)}, u32[]{:S(2)}) copy-start(bf16[2048,128]{1,0:T(8,128)(2,1)} %param.16) | copy-start | bytes 1572868
  92.1 6.0 %collective-permute-start.6 = (bf16[7,2048]{1,0:T(8,128)(2,1)S(1)}, bf16[7,2048]{1,0:T(8,128)(2,1)S(1)}, u32[]{:S(2)}, u32[]{:S(2)}) collective-permute-start(bf16[7,2048]{1,0:T(8,128)(2,1)S(1)} %slice.24), channel_id=1, source_target_pairs={{0,1},{1,2},{2,3},{3,4},{4,5},{5,6},{6,7},{7,8},{8,9},{9,10},{10,1... | collective-permute-start | bytes 86024 | tf_op jit(solution)/shard_map/ppermute | solution.py:49
  108.8 35.4 %collective-permute-start.7 = (bf16[96,128]{1,0:T(8,128)(2,1)S(1)}, bf16[96,128]{1,0:T(8,128)(2,1)S(1)}, u32[]{:S(2)}, u32[]{:S(2)}) collective-permute-start(bf16[96,128]{1,0:T(8,128)(2,1)S(1)} %get-tuple-element.5), channel_id=1, source_target_pairs={{0,4},{4,8},{8,12},{12,16},{16,20},{20,24},{24,28},{28,0},{1,5},{5... | collective-permute-start | bytes 73736 | tf_op jit(solution)/shard_map/ppermute | solution.py:33
  110.4 33.9 %collective-permute-start.8 = (bf16[96,128]{1,0:T(8,128)(2,1)S(1)}, bf16[96,128]{1,0:T(8,128)(2,1)S(1)}, u32[]{:S(2)}, u32[]{:S(2)}) collective-permute-start(bf16[96,128]{1,0:T(8,128)(2,1)S(1)} %get-tuple-element.5), channel_id=1, source_target_pairs={{0,28},{4,0},{8,4},{12,8},{16,12},{20,16},{24,20},{28,24},{1,29},{... | collective-permute-start | bytes 73736 | tf_op jit(solution)/shard_map/ppermute | solution.py:38
  144.2 6.5 %collective-permute-start.9 = (bf16[96,128]{1,0:T(8,128)(2,1)S(1)}, bf16[96,128]{1,0:T(8,128)(2,1)S(1)}, u32[]{:S(2)}, u32[]{:S(2)}) collective-permute-start(bf16[96,128]{1,0:T(8,128)(2,1)S(1)} %collective-permute-done.7), channel_id=1, source_target_pairs={{0,4},{4,8},{8,12},{12,16},{16,20},{20,24},{24,28},{28,0},{1,5},{5... | collective-permute-start | bytes 73736 | tf_op jit(solution)/shard_map/ppermute | solution.py:33
  144.2 6.5 %collective-permute-start.10 = (bf16[96,128]{1,0:T(8,128)(2,1)S(1)}, bf16[96,128]{1,0:T(8,128)(2,1)S(1)}, u32[]{:S(2)}, u32[]{:S(2)}) collective-permute-start(bf16[96,128]{1,0:T(8,128)(2,1)S(1)} %collective-permute-done.8), channel_id=1, source_target_pairs={{0,28},{4,0},{8,4},{12,8},{16,12},{20,16},{24,20},{28,24},{1,29},{... | collective-permute-start | bytes 73736 | tf_op jit(solution)/shard_map/ppermute | solution.py:38
  150.7 6.5 %collective-permute-start.11 = (bf16[96,128]{1,0:T(8,128)(2,1)S(1)}, bf16[96,128]{1,0:T(8,128)(2,1)S(1)}, u32[]{:S(2)}, u32[]{:S(2)}) collective-permute-start(bf16[96,128]{1,0:T(8,128)(2,1)S(1)} %collective-permute-done.9), channel_id=1, source_target_pairs={{0,4},{4,8},{8,12},{12,16},{16,20},{20,24},{24,28},{28,0},{1,5},{5... | collective-permute-start | bytes 73736 | tf_op jit(solution)/shard_map/ppermute | solution.py:33
  150.8 6.5 %collective-permute-start.12 = (bf16[96,128]{1,0:T(8,128)(2,1)S(1)}, bf16[96,128]{1,0:T(8,128)(2,1)S(1)}, u32[]{:S(2)}, u32[]{:S(2)}) collective-permute-start(bf16[96,128]{1,0:T(8,128)(2,1)S(1)} %collective-permute-done.10), channel_id=1, source_target_pairs={{0,28},{4,0},{8,4},{12,8},{16,12},{20,16},{24,20},{28,24},{1,29},{... | collective-permute-start | bytes 73736 | tf_op jit(solution)/shard_map/ppermute | solution.py:38
  157.3 6.5 %collective-permute-start.13 = (bf16[96,128]{1,0:T(8,128)(2,1)S(1)}, bf16[96,128]{1,0:T(8,128)(2,1)S(1)}, u32[]{:S(2)}, u32[]{:S(2)}) collective-permute-start(bf16[96,128]{1,0:T(8,128)(2,1)S(1)} %collective-permute-done.11), channel_id=1, source_target_pairs={{0,4},{4,8},{8,12},{12,16},{16,20},{20,24},{24,28},{28,0},{1,5},{5... | collective-permute-start | bytes 73736 | tf_op jit(solution)/shard_map/ppermute | solution.py:33
Sparse Core Ops, SparseCore 0:
  8.9 56.0 all-gather.1
  165.8 17.7 reduce-scatter.1
